TPU v7x, 32 devices: a whole 2x2x4 slice. The times are simulated.
32 devices in a mesh: groups: 2 (over x), roll: 8 (over z, y), width: 2 (over core).
Axes of the slice: x: 2, y: 2, z: 4, core: 2. Of those that a mesh axis runs over, the one named last changes fastest.
Arguments:
- lines_y: bfloat16 [1792, 16384], P(('groups', 'roll'), 'width'), parts along dimension 0, may hold values from -96 to 96
- defect_mask: int32 [1792, 128], P(('groups', 'roll'), 'width'), parts along dimension 0, may hold values from 0 to 1
- loading: bfloat16 [16384, 128], P('width'), may hold values from -17 to 17
- decay_rate: float32 [64], replicated, may hold values from 1e-05 to 0.03
- angle: float32 [64], replicated, may hold values from -3.140625 to 3.140625
- gain: float32 [64], replicated, may hold values from 0.0003 to 0.009
- smooth_gain: float32 [64], replicated, may hold values from 0.3 to 0.9998
- initial: float32 [256], P('groups'), parts along dimension 0, may hold values from -4 to 4
Outputs:
- smoothed: float32 [1792, 128], P(('groups', 'roll')), parts along dimension 0
- background: bfloat16 [1792, 16384], P(('groups', 'roll'), 'width'), parts along dimension 0
There are 2 independent parts, one for each index of `groups`. A program takes and returns all parts, laid end to end along the dimension named above; an argument that names none is the same for every part. Nothing has to cross between parts.
All inputs are finite; a program needn't handle non-finite values.
Results may differ from a plain program's by a relative error of at most 0.0049.
Values sent between devices are 32-bit elements; how exact they have to be, the bound alone decides.
A program may use at most 64 MiB of HBM per device.

v0:
```python
import math

import jax
import jax.numpy as jnp
from jax import lax
from jax.sharding import PartitionSpec as P

PIX_BLK = 128


precise_mode = lax.Precision.HIGHEST


def entering(part, axis, combine, identity, reverse):
    count = lax.axis_size(axis)
    place = lax.axis_index(axis)
    ahead = count - 1 - place if reverse else place
    gathered = jax.tree.map(lambda a: lax.all_gather(a, axis), part)
    state = jax.tree.map(lambda a, e: jnp.zeros_like(a) + jnp.asarray(e, a.dtype), part, identity)

    def one(hop, state):
        source = count - 1 - hop if reverse else hop
        return combine(
            state, jax.tree.map(lambda a: lax.dynamic_index_in_dim(a, source, 0, False), gathered)
        )

    return lax.fori_loop(0, ahead, one, state)


def chain_up(matrices, offsets):
    levels = [(matrices, offsets)]
    while matrices.shape[0] > 1:
        count = matrices.shape[0]
        pairs = count // 2
        early_m = matrices[0 : 2 * pairs : 2]
        late_m = matrices[1 : 2 * pairs : 2]
        joined_m = jnp.einsum("nij,njk->nik", late_m, early_m, precision=precise_mode)
        joined_g = (
            jnp.einsum("nij,nj->ni", late_m, offsets[0 : 2 * pairs : 2], precision=precise_mode)
            + offsets[1 : 2 * pairs : 2]
        )
        if count % 2 == 1:
            joined_m = jnp.concatenate([joined_m, matrices[count - 1 :]], axis=0)
            joined_g = jnp.concatenate([joined_g, offsets[count - 1 :]], axis=0)
        matrices, offsets = (joined_m, joined_g)
        levels.append((matrices, offsets))
    return levels


def chain_down(levels, start):
    top_m, top_g = levels[-1]
    states = (jnp.dot(top_m[0], start, precision=precise_mode) + top_g[0])[None]
    for matrices, offsets in reversed(levels[:-1]):
        count = matrices.shape[0]
        pairs = count // 2
        prior = jnp.concatenate([start[None], states[: pairs - 1]], axis=0)
        evens = (
            jnp.einsum("nij,nj->ni", matrices[0 : 2 * pairs : 2], prior, precision=precise_mode)
            + offsets[0 : 2 * pairs : 2]
        )
        paired = jnp.stack([evens, states[:pairs]], axis=1).reshape(2 * pairs, -1)
        if count % 2 == 1:
            paired = jnp.concatenate([paired, states[pairs : pairs + 1]], axis=0)
        states = paired
    return states


def join_ahead(earlier, later):
    joined_m = jnp.dot(later[0], earlier[0], precision=precise_mode)
    joined_g = jnp.dot(later[0], earlier[1], precision=precise_mode) + later[1]
    return (joined_m, joined_g)


def join_back(first, second):
    width_half = first[0].shape[-1]
    real_a, imag_a, off_a = first
    real_b, imag_b, off_b = second
    real_c = real_b * real_a - imag_b * imag_a
    imag_c = real_b * imag_a + imag_b * real_a
    off_re = (
        real_b * off_a[..., :width_half]
        - imag_b * off_a[..., width_half:]
        + off_b[..., :width_half]
    )
    off_im = (
        real_b * off_a[..., width_half:]
        + imag_b * off_a[..., :width_half]
        + off_b[..., width_half:]
    )
    return (real_c, imag_c, jnp.concatenate([off_re, off_im], axis=-1))


def shards(lines_y, defect_mask, loading, decay_rate, angle, gain, smooth_gain, initial):
    states_dim = loading.shape[1]
    width_half = states_dim // 2
    local_pixels = lines_y.shape[1]
    pixels = local_pixels * lax.axis_size("width")
    local_blocks = local_pixels // PIX_BLK
    radius = 1.0 - decay_rate
    cos_part = radius * jnp.cos(angle)
    sin_part = radius * jnp.sin(angle)
    gain_full = jnp.concatenate([gain, gain])
    keep_part = 1.0 - smooth_gain * radius * radius
    keep_full = jnp.concatenate([keep_part, keep_part])
    masked = lines_y * jnp.repeat(defect_mask.astype(jnp.bfloat16), PIX_BLK, axis=1)
    proj_part = jnp.dot(masked, loading, preferred_element_type=jnp.float32) * (
        math.sqrt(states_dim) / pixels
    )
    pieces = loading.reshape(local_blocks, PIX_BLK, states_dim)
    block_gram = jnp.einsum(
        "bps,bpt->bst", pieces, pieces, preferred_element_type=jnp.float32
    ).reshape(local_blocks, states_dim * states_dim)
    mask_f = defect_mask.astype(jnp.float32)
    gram_part = jnp.dot(mask_f, block_gram, precision=precise_mode) / pixels
    gram_rows, projected = lax.psum((gram_part, proj_part), "width")
    count = gram_rows.shape[0]
    grams = gram_rows.reshape(count, states_dim, states_dim)
    left_cols = grams[:, :, :width_half]
    right_cols = grams[:, :, width_half:]
    times_a = jnp.concatenate(
        [
            left_cols * cos_part + right_cols * sin_part,
            right_cols * cos_part - left_cols * sin_part,
        ],
        axis=2,
    )
    top_rows = jnp.concatenate([jnp.diag(cos_part), -jnp.diag(sin_part)], axis=1)
    bottom_rows = jnp.concatenate([jnp.diag(sin_part), jnp.diag(cos_part)], axis=1)
    dense_a = jnp.concatenate([top_rows, bottom_rows], axis=0)
    matrices = dense_a[None] - gain_full[None, :, None] * times_a
    offsets = gain_full * projected
    levels = chain_up(matrices, offsets)
    whole_m = levels[-1][0][0]
    whole_g = levels[-1][1][0]
    identity_f = (jnp.eye(states_dim, dtype=jnp.float32), jnp.zeros((states_dim,), jnp.float32))
    prior_m, prior_g = entering((whole_m, whole_g), "roll", join_ahead, identity_f, False)
    first_line = lax.axis_index("roll") * count
    total_lines = count * lax.axis_size("roll")
    start = jnp.dot(prior_m, initial, precision=precise_mode) + prior_g
    filtered = chain_down(levels, start)
    is_last = first_line + jnp.arange(count, dtype=jnp.int32) == total_lines - 1
    zero_f = jnp.zeros((count, width_half), jnp.float32)
    coef_re = jnp.where(is_last[:, None], zero_f, (smooth_gain * cos_part)[None] + zero_f)
    coef_im = jnp.where(is_last[:, None], zero_f, -(smooth_gain * sin_part)[None] + zero_f)
    off_terms = jnp.where(is_last[:, None], filtered, keep_full * filtered)
    flipped = (jnp.flip(coef_re, 0), jnp.flip(coef_im, 0), jnp.flip(off_terms, 0))
    acc_re, acc_im, acc_off = lax.associative_scan(join_back, flipped)
    whole_b = (acc_re[count - 1], acc_im[count - 1], acc_off[count - 1])
    identity_b = (
        jnp.ones((width_half,), jnp.float32),
        jnp.zeros((width_half,), jnp.float32),
        jnp.zeros((states_dim,), jnp.float32),
    )
    after = entering(whole_b, "roll", join_back, identity_b, True)
    real_in = after[2][:width_half]
    imag_in = after[2][width_half:]
    smooth_re = acc_re * real_in - acc_im * imag_in + acc_off[:, :width_half]
    smooth_im = acc_re * imag_in + acc_im * real_in + acc_off[:, width_half:]
    smoothed = jnp.flip(jnp.concatenate([smooth_re, smooth_im], axis=1), 0)
    image_rows = lax.dot_general(
        smoothed.astype(jnp.bfloat16),
        loading,
        (((1,), (1,)), ((), ())),
        preferred_element_type=jnp.float32,
    )
    background = (image_rows * (1.0 / math.sqrt(states_dim))).astype(jnp.bfloat16)
    return (smoothed, background)


def solution(mesh):
    in_specs = (
        P(("groups", "roll"), "width"),
        P(("groups", "roll"), "width"),
        P("width", None),
        P(),
        P(),
        P(),
        P(),
        P("groups"),
    )
    out_specs = (P(("groups", "roll"), None), P(("groups", "roll"), "width"))
    return jax.shard_map(shards, mesh=mesh, in_specs=in_specs, out_specs=out_specs, check_vma=False)
```

profile of v0, /device:TPU:0, one launch (start us, length us, event | category | flops | bytes accessed | tf_op | source)
XLA Modules:
  0.0 292.0 jit_solution(4536561667060600960)
XLA Ops:
  7.2 1.5 copy-done
  9.6 8.5 %fusion.22 = f32[14,8,128,128]{3,1,2,0:T(8,128)S(1)} fusion(f32[8,8,128,128]{3,2,1,0:T(8,128)S(1)} %bitcast.211, s32[112,64]{0,1:T(8,128)S(1)} %copy-done.11), kind=kOutput, calls=%fused_computation.34 | convolution fusion | flops 1411128320 | bytes 11563008 | tf_op jit(solution)/shard_map/dot_general | solution.py:114
  18.2 4.3 %copy.60 = f32[14,8,128,128]{3,2,1,0:T(8,128)} copy(f32[14,8,128,128]{3,1,2,0:T(8,128)S(1)} %fusion.22) | data formatting | bytes 14680064
  22.7 1.4 broadcast_in_dim.93
  24.0 3.0 %fusion.34 = f32[112,128]{1,0:T(8,128)S(1)} fusion(bf16[8192,128]{1,0:T(8,128)(2,1)S(1)} %copy-done, bf16[112,8192]{1,0:T(8,128)(2,1)} %param.12, bf16[14,8,64,128]{3,2,1,0:T(8,128)(2,1)S(1)} %bitcast.212), kind=kOutput, calls=%fused_computation.45 | convolution fusion | flops 235812864 | bytes 5824512 | tf_op jit(solution)/shard_map/dot_general | solution.py:106
  27.0 3.9 %psum.15 = f32[112,128]{1,0:T(8,128)S(1)} all-reduce(f32[112,128]{1,0:T(8,128)S(1)} %fusion.34), channel_id=1, replica_groups=mesh['groups'=2,'roll'=8,'width'=2] {'width'}, use_global_device_ids=true, to_apply=%region_1.0 | all-reduce | flops 14336 | bytes 114688 | tf_op jit(solution)/shard_map/psum | solution.py:115
  37.2 22.2 %all-reduce.38.cloned.1.call-done = f32[112,128,128]{2,1,0:T(8,128)} async-done(((f32[112,128,128]{2,1,0:T(8,128)}), f32[112,128,128]{2,1,0:T(8,128)}) %all-reduce.38.cloned.1.call-update) | async-done | bytes 7340048 | tf_op jit(solution)/shard_map/psum | solution.py:115
  59.4 7.8 %multiply_add_fusion = (f32[112,128,64]{2,1,0:T(8,128)S(1)}, f32[112,128,64]{2,1,0:T(8,128)S(1)}) fusion(f32[112,128,128]{2,1,0:T(8,128)} %all-reduce.38.cloned.1.call-done, f32[64]{0:T(128)S(1)} %get-tuple-element.247, f32[64]{0:T(128)S(1)} %get-tuple-element.175), kind=kLoop, calls=%fused_computation.24 | loop fusion | flops 5505024 | bytes 14680576 | tf_op jit(solution)/shard_map/add | solution.py:122
  67.2 2.1 fusion.12
  69.4 5.9 %fusion.17 = f32[56,128,128]{2,1,0:T(8,128)} fusion(f32[112,128,128]{2,1,0:T(8,128)S(1)} %fusion.12), kind=kOutput, calls=%fused_computation.29 | convolution fusion | flops 1409286144 | bytes 11010048 | tf_op jit(solution)/shard_map/nij,njk->nik/dot_general | solution.py:37
  75.3 5.8 %fusion.15 = f32[56,1,128]{2,1,0:T(1,128)S(1)} fusion(f32[56,128,1]{1,2,0:T(1,128)S(1)} %bitcast.214, f32[112,128,128]{2,1,0:T(8,128)S(1)} %fusion.12), kind=kOutput, calls=%fused_computation.27 | convolution fusion | flops 11010048 | bytes 3727360 | tf_op jit(solution)/shard_map/nij,nj->ni/dot_general | solution.py:39
  81.1 5.3 %fusion.29 = f32[28,128,128]{2,1,0:T(8,128)} fusion(f32[56,128,128]{2,1,0:T(8,128)} %fusion.17), kind=kOutput, calls=%fused_computation.40 | convolution fusion | flops 704643072 | bytes 5505024 | tf_op jit(solution)/shard_map/nij,njk->nik/dot_general | solution.py:37
  86.4 2.9 %fusion.31 = f32[28,1,128]{2,1,0:T(1,128)S(1)} fusion(f32[56,128,128]{2,1,0:T(8,128)S(1)} %copy-done.2, f32[28,128,1]{1,0,2:T(8,128)S(1)} %bitcast.218), kind=kOutput, calls=%fused_computation.42 | convolution fusion | flops 5505024 | bytes 1865728 | tf_op jit(solution)/shard_map/nij,nj->ni/dot_general | solution.py:39
  89.4 13.1 %fusion.40 = f32[14,128,128]{2,1,0:T(8,128)S(1)} fusion(f32[28,128,128]{2,1,0:T(8,128)} %fusion.29), kind=kOutput, calls=%fused_computation.55 | convolution fusion | flops 352321536 | bytes 2752512 | tf_op jit(solution)/shard_map/nij,njk->nik/dot_general | solution.py:37
  102.6 2.7 fusion.42
  107.1 1.5 fusion.49
  108.6 1.3 bitcast_add_fusion.7
  109.9 1.3 slice.746
  111.1 1.3 slice.747
  117.1 1.2 slice.749
  118.3 1.3 slice.750
  123.2 21.6 %all-gather.3 = f32[8,1,128]{2,1,0:T(1,128)} all-gather(f32[1,1,128]{2,1,0:T(1,128)S(1)} %bitcast.239), channel_id=1, replica_groups=mesh['groups'=2,'roll'=8,'width'=2] {'roll'}, dimensions={0}, use_global_device_ids=true | all-gather | bytes 4608 | tf_op jit(solution)/shard_map/all_gather | solution.py:18
  144.8 33.4 %all-gather = f32[1024,128]{1,0:T(8,128)} all-gather(f32[128,128]{1,0:T(8,128)S(1)} %fusion.67), channel_id=2, replica_groups=mesh['groups'=2,'roll'=8,'width'=2] {'roll'}, dimensions={0}, use_global_device_ids=true | all-gather | bytes 589824 | tf_op jit(solution)/shard_map/all_gather | solution.py:18
  181.7 1.2 fusion.59
  187.7 2.7 fusion.38
  191.9 4.4 %fusion.27 = f32[28,1,128]{2,1,0:T(1,128)S(1)} fusion(f32[56,128,128]{2,1,0:T(8,128)} %fusion.17, f32[28,128,1]{1,0,2:T(8,128)S(1)} %maximum_bitcast_fusion), kind=kOutput, calls=%fused_computation.38 | convolution fusion | flops 5505024 | bytes 1863680 | tf_op jit(solution)/shard_map/nij,nj->ni/dot_general | solution.py:58
  196.4 7.8 %fusion.19 = f32[56,1,128]{2,1,0:T(1,128)S(1)} fusion(f32[56,128,1]{1,2,0:T(1,128)S(1)} %bitcast.219, f32[112,128,128]{2,1,0:T(8,128)} %copy-done.1), kind=kOutput, calls=%fused_computation.31 | convolution fusion | flops 11010048 | bytes 3727360 | tf_op jit(solution)/shard_map/nij,nj->ni/dot_general | solution.py:58
  208.3 38.9 %all-gather.4 = f32[8,1,128]{2,1,0:T(1,128)S(1)} all-gather(f32[1,1,128]{2,1,0:T(1,128)S(1)} %add_bitcast_fusion.2), channel_id=1, replica_groups=mesh['groups'=2,'roll'=8,'width'=2] {'roll'}, dimensions={0}, use_global_device_ids=true | all-gather | bytes 4608 | tf_op jit(solution)/shard_map/all_gather | solution.py:18
  247.2 16.2 %all-gather.2 = f32[8,1,64]{2,1,0:T(1,128)S(1)} all-gather(f32[1,1,64]{2,1,0:T(1,128)S(1)} %add_bitcast_fusion.3), channel_id=1, replica_groups=mesh['groups'=2,'roll'=8,'width'=2] {'roll'}, dimensions={0}, use_global_device_ids=true | all-gather | bytes 2304 | tf_op jit(solution)/shard_map/all_gather | solution.py:18
  263.4 18.2 %all-gather.1 = f32[8,1,64]{2,1,0:T(1,128)S(1)} all-gather(f32[1,1,64]{2,1,0:T(1,128)S(1)} %add_bitcast_fusion.4), channel_id=1, replica_groups=mesh['groups'=2,'roll'=8,'width'=2] {'roll'}, dimensions={0}, use_global_device_ids=true | all-gather | bytes 2304 | tf_op jit(solution)/shard_map/all_gather | solution.py:18
  281.6 1.1 while.28
  283.1 2.0 fusion.11
  (329 shorter events, 32.2 us)
Async XLA Ops:
  7.2 1.6 copy-start
  7.2 52.2 %all-reduce.38.cloned.1.call-start = ((), (), s32[]{:S(2)}) async-start(), calls=%async_computation | async-start | bytes 14680064 | tf_op jit(solution)/shard_map/psum | solution.py:115
  8.8 0.9 copy-start.11
  22.6 8.3 %copy-start.29 = (f32[64]{0:T(128)S(1)}, f32[64]{0:T(128)}, u32[]{:S(2)}) copy-start(f32[64]{0:T(128)} %param.17) | copy-start | bytes 772
  22.6 8.4 %copy-start.26 = (f32[64]{0:T(128)S(1)}, f32[64]{0:T(128)}, u32[]{:S(2)}) copy-start(f32[64]{0:T(128)} %param.18) | copy-start | bytes 772
  22.6 8.4 %copy-start.27 = (f32[64]{0:T(128)S(1)}, f32[64]{0:T(128)}, u32[]{:S(2)}) copy-start(f32[64]{0:T(128)} %param.16) | copy-start | bytes 772
  22.7 8.4 %copy-start.28 = (f32[64]{0:T(128)S(1)}, f32[64]{0:T(128)}, u32[]{:S(2)}) copy-start(f32[64]{0:T(128)} %param.15) | copy-start | bytes 772
  31.0 44.3 %copy-start.6 = (f32[56,128]{1,0:T(8,128)}, f32[56,128]{1,0:T(8,128)S(1)}, u32[]{:S(2)}) copy-start(f32[56,128]{1,0:T(8,128)S(1)} %slice.738) | copy-start | bytes 86020
  31.1 0.5 copy-start.21
  69.3 5.9 %copy-start.1 = (f32[112,128,128]{2,1,0:T(8,128)}, f32[112,128,128]{2,1,0:T(8,128)S(1)}, u32[]{:S(2)}) copy-start(f32[112,128,128]{2,1,0:T(8,128)S(1)} %fusion.12) | copy-start | bytes 22020100
  81.1 5.3 %copy-start.2 = (f32[56,128,128]{2,1,0:T(8,128)S(1)}, f32[56,128,128]{2,1,0:T(8,128)}, u32[]{:S(2)}) copy-start(f32[56,128,128]{2,1,0:T(8,128)} %fusion.17) | copy-start | bytes 11010052
  89.4 16.5 %copy-start.16 = (f32[14,128]{1,0:T(8,128)}, f32[14,128]{1,0:T(8,128)S(1)}, u32[]{:S(2)}) copy-start(f32[14,128]{1,0:T(8,128)S(1)} %slice.742) | copy-start | bytes 21508
  120.5 0.7 copy-start.3
  120.8 2.3 copy-start.4
  122.4 22.5 %copy-start.5 = (f32[128,128]{1,0:T(8,128)}, f32[128,128]{1,0:T(8,128)S(1)}, u32[]{:S(2)}) copy-start(f32[128,128]{1,0:T(8,128)S(1)} %fusion.67) | copy-start | bytes 196612
  123.1 55.1 %copy-start.19 = (f32[2,128]{1,0:T(2,128)}, f32[2,128]{1,0:T(2,128)S(1)}, u32[]{:S(2)}) copy-start(f32[2,128]{1,0:T(2,128)S(1)} %add.440) | copy-start | bytes 3076
  123.2 55.0 %copy-start.20 = (f32[1,128]{1,0:T(1,128)}, f32[1,128]{1,0:T(1,128)S(1)}, u32[]{:S(2)}) copy-start(f32[1,128]{1,0:T(1,128)S(1)} %convolution_add_fusion.1) | copy-start | bytes 1540
  179.5 4.5 %copy-start.17 = (f32[128]{0:T(128)}, f32[128]{0:T(128)S(1)}, u32[]{:S(2)}) copy-start(f32[128]{0:T(128)S(1)} %fusion.37) | copy-start | bytes 1540
  184.1 12.3 %copy-start.18 = (f32[128]{0:T(128)S(1)}, f32[128]{0:T(128)}, u32[]{:S(2)}) copy-start(f32[128]{0:T(128)} %copy-done.17) | copy-start | bytes 1540
  185.5 18.8 %copy-start.7 = (f32[56,128]{1,0:T(8,128)S(1)}, f32[56,128]{1,0:T(8,128)}, u32[]{:S(2)}) copy-start(f32[56,128]{1,0:T(8,128)} %copy-done.6) | copy-start | bytes 86020
  187.0 17.4 %copy-start.22 = (pred[112]{0:T(512)(128)(4,1)S(1)}, pred[112]{0:T(512)(128)(4,1)}, u32[]{:S(2)}) copy-start(pred[112]{0:T(512)(128)(4,1)} %copy-done.21) | copy-start | bytes 340
  187.0 17.4 %copy-start.25 = (f32[128]{0:T(128)S(1)}, f32[128]{0:T(128)}, u32[]{:S(2)}) copy-start(f32[128]{0:T(128)} %pad_maximum_fusion.30) | copy-start | bytes 1540
  190.4 14.3 %copy-start.12 = (f32[56,64]{1,0:T(8,128)S(1)}, f32[56,64]{1,0:T(8,128)}, u32[]{:S(2)}) copy-start(f32[56,64]{1,0:T(8,128)} %slice.663) | copy-start | bytes 43012
  190.4 14.3 %copy-start.13 = (f32[56,64]{1,0:T(8,128)S(1)}, f32[56,64]{1,0:T(8,128)}, u32[]{:S(2)}) copy-start(f32[56,64]{1,0:T(8,128)} %slice.665) | copy-start | bytes 43012
  190.4 14.3 %copy-start.14 = (f32[56,64]{1,0:T(8,128)S(1)}, f32[56,64]{1,0:T(8,128)}, u32[]{:S(2)}) copy-start(f32[56,64]{1,0:T(8,128)} %slice.667) | copy-start | bytes 43012
  190.4 14.3 %copy-start.15 = (f32[56,64]{1,0:T(8,128)S(1)}, f32[56,64]{1,0:T(8,128)}, u32[]{:S(2)}) copy-start(f32[56,64]{1,0:T(8,128)} %slice.669) | copy-start | bytes 43012
  196.4 11.6 %copy-start.8 = (f32[55,64]{1,0:T(8,128)S(1)}, f32[55,64]{1,0:T(8,128)}, u32[]{:S(2)}) copy-start(f32[55,64]{1,0:T(8,128)} %slice.661) | copy-start | bytes 42244
  196.4 11.6 %copy-start.9 = (f32[55,64]{1,0:T(8,128)S(1)}, f32[55,64]{1,0:T(8,128)}, u32[]{:S(2)}) copy-start(f32[55,64]{1,0:T(8,128)} %slice.715) | copy-start | bytes 42244
  204.3 42.9 %copy-start.24 = (f32[1,64]{1,0:T(1,128)S(1)}, f32[1,64]{1,0:T(1,128)}, u32[]{:S(2)}) copy-start(f32[1,64]{1,0:T(1,128)} %slice.859) | copy-start | bytes 772
  204.3 59.1 %copy-start.23 = (f32[1,64]{1,0:T(1,128)S(1)}, f32[1,64]{1,0:T(1,128)}, u32[]{:S(2)}) copy-start(f32[1,64]{1,0:T(1,128)} %slice.838) | copy-start | bytes 772
  283.0 2.0 copy-start.10
Sparse Core Ops, SparseCore 0:
  22.6 36.7 all-reduce.37
where the time goes:
time: 296 us; the launch traced here: 292 us
  blocking collectives  132 us (45%)
  matrix products  76.1 us (26%)
  other arithmetic  23.7 us (8%)
  local copies, waits for them, and re-layouts  22.6 us (8%)
  waiting for transfers between devices  22.2 us (8%)
  between operations  15.3 us (5%)
    all_gather x5, blocking collectives, entering(): gathered = jax.tree.map(lambda a: lax.all_gather(a, axis), part)  128 us
    dot_general x7, matrix products, chain_up(): jnp.einsum('nij,njk->nik', late_m, early_m, precision=precise_mode)  26.4 us
    psum x1, waiting for transfers between devices, shards(): gram_rows, projected = lax.psum((gram_part, proj_part), 'width')  22.2 us
    dot_general x7, matrix products, chain_down(): jnp.einsum('nij,nj->ni', matrices[0:2 * pairs:2], prior, precision=precis...  18.4 us
    dot_general x7, matrix products, chain_up(): jnp.einsum('nij,nj->ni', late_m, offsets[0:2 * pairs:2], precision=precis...  15.1 us
    dot_general x1, matrix products, shards(): gram_part = jnp.dot(mask_f, block_gram, precision=precise_mode) / pixels  8.53 us
    add x1, other arithmetic, shards(): left_cols * cos_part + right_cols * sin_part  7.83 us
    unnamed x63, local copies, waits for them, and re-layouts  6.73 us
  transfers between devices with their start and end apart: 1, of which 1 were waited for; matrix products, arithmetic and copies ran while one was open for 4% of the time, Pallas kernels for 0%

commit v1 on v0

v1 whole, which is shorter than its diff:
```python
import functools
import math

import jax
import jax.numpy as jnp
from jax import lax
from jax.experimental import pallas as pl
from jax.experimental.pallas import tpu as pltpu
from jax.sharding import PartitionSpec as P

PIX_BLK = 128
CHAINS = 8
PIECES = 8
MESH = pl.DeviceIdType.MESH
HI = lax.Precision.HIGHEST
F32 = jnp.float32
BF16 = jnp.bfloat16


def turn(v):
    return pltpu.roll(v, v.shape[-1] // 2, 1)


def join(first, second, dst):
    s = second.shape[1]
    r = jnp.dot(first, second[:s], precision=HI, preferred_element_type=F32)
    dst[0:s, :] = r[:s]
    dst[s : s + 8, :] = r[s:] + second[s:]


def column(x):
    return jnp.broadcast_to(x, (x.shape[1], x.shape[1])).T


def apply(xcol, m):
    s = xcol.shape[0]
    return jnp.sum(m[:s] * xcol, axis=0, keepdims=True) + m[s : s + 1]


def powers(fr, fi, expo, bits):
    tr = jnp.ones(expo.shape, F32)
    ti = jnp.zeros(expo.shape, F32)
    for k in range(bits):
        on = (expo >> k) & 1 == 1
        nr = tr * fr - ti * fi
        ni = tr * fi + ti * fr
        tr = jnp.where(on, nr, tr)
        ti = jnp.where(on, ni, ti)
        fr, fi = fr * fr - fi * fi, 2.0 * fr * fi
    return tr, ti


def kernel(
    n_roll, y_ref, mask_ref, load_ref, par_ref, init_ref, out_ref,
    bs, gsend, gown, grecv, pacc, precv, pown, pall, comb, mcore, mpair, mquad, mrecv, xs,
    xsend, xrecv, bsend, brecv, ssend, srecv,
    g_ss, g_rs, one_ss, one_rs, b_ss, b_rs,
):
    s = load_ref.shape[1]
    lines = y_ref.shape[0]
    th = lines // 2
    steps = th // CHAINS
    nb = load_ref.shape[0] // PIX_BLK
    nq = 2 * n_roll
    r = lax.axis_index("roll")
    w = lax.axis_index("width")
    q = 2 * r + w
    other = 1 - w

    def at(place):
        return {"roll": lax.div(place, 2), "width": lax.rem(place, 2)}

    barrier = pltpu.get_barrier_semaphore()

    def greet(d, _):
        pl.semaphore_signal(barrier, inc=1, device_id=at(lax.rem(q + d, nq)), device_id_type=MESH)
        return 0

    lax.fori_loop(1, nq, greet, 0)

    cosd = par_ref[0:1, :]
    sind = par_ref[1:2, :]
    kap_g = par_ref[2:3, :]
    kap_p = par_ref[3:4, :]
    fr = par_ref[4:5, :]
    fi = par_ref[5:6, :]
    keep = par_ref[6:7, :]
    sgn = par_ref[7:8, :]

    own_rows = pl.ds(pl.multiple_of(w * th, 8), th)
    oth_rows = pl.ds(pl.multiple_of(other * th, 8), th)
    m_all = mask_ref[...].astype(F32).astype(BF16)
    m_two = jnp.concatenate(
        [mask_ref[oth_rows, :].astype(F32), mask_ref[own_rows, :].astype(F32)], axis=0
    ).astype(BF16)

    pacc[...] = jnp.zeros_like(pacc)
    per = 4

    def blocks(g, _):
        total = pacc[...]
        for k in range(per):
            b = g * per + k
            rows = pl.ds(pl.multiple_of(b * PIX_BLK, PIX_BLK), PIX_BLK)
            h = load_ref[rows, :]
            bs[pl.ds(pl.multiple_of(b * s, s), s), :] = lax.dot_general(
                h, h, (((0,), (0,)), ((), ())), preferred_element_type=F32
            )
            pick = jnp.where(lax.broadcasted_iota(jnp.int32, (nb, PIX_BLK), 0) == b, 1.0, 0.0).astype(BF16)
            mb = jnp.dot(m_all, pick, preferred_element_type=F32)
            my = (y_ref[:, rows].astype(F32) * mb).astype(BF16)
            total += jnp.dot(my, h, preferred_element_type=F32)
        pacc[...] = total
        return 0

    lax.fori_loop(0, nb // per, blocks, 0)

    pl.semaphore_wait(barrier, nq - 1)

    def exchange(src, dst, k, dev):
        return pltpu.make_async_remote_copy(
            src_ref=src, dst_ref=dst, send_sem=one_ss.at[k], recv_sem=one_rs.at[k],
            device_id=dev, device_id_type=MESH,
        )

    partner = {"roll": r, "width": other}
    c_proj = exchange(pacc.at[oth_rows, :], precv, 0, partner)
    c_proj.start()

    piece = s // PIECES
    copies = []
    for c in range(PIECES):
        def rows_of(g, _):
            for k in range(per):
                i = c * piece + g * per + k
                bi = bs[pl.ds(i, nb, stride=s), :].astype(BF16)
                res = jnp.dot(m_two, bi, preferred_element_type=F32)
                dst = pl.ds(pl.multiple_of(i * th, 8), th)
                gsend[dst, :] = res[:th]
                gown[dst, :] = res[th:]
            return 0

        lax.fori_loop(0, piece // per, rows_of, 0)
        span = pl.ds(c * piece * th, piece * th)
        cp = pltpu.make_async_remote_copy(
            src_ref=gsend.at[span, :], dst_ref=grecv.at[span, :], send_sem=g_ss.at[c],
            recv_sem=g_rs.at[c], device_id=partner, device_id_type=MESH,
        )
        cp.start()
        copies.append(cp)

    row_t = lax.broadcasted_iota(jnp.int32, (th, s), 0)
    tail_r, tail_i = powers(fr, fi, th - row_t, th.bit_length())
    far_r, far_i = powers(
        tail_r[0:1], tail_i[0:1], lax.broadcasted_iota(jnp.int32, (nq, s), 0), nq.bit_length()
    )

    ident = jnp.where(
        lax.broadcasted_iota(jnp.int32, (s + 8, s), 0) == lax.broadcasted_iota(jnp.int32, (s + 8, s), 1),
        1.0, 0.0,
    )
    for c in range(CHAINS):
        pall[c * (steps + 1)] = ident

    c_proj.wait()
    pown[...] = (pacc[own_rows, :] + precv[...]) * kap_p
    for cp in copies:
        cp.wait()

    def step(k, _):
        for c in range(CHAINS):
            t = c * steps + k
            gram = (gown[pl.ds(t, s, stride=th), :] + grecv[pl.ds(t, s, stride=th), :]).astype(BF16)
            p = pall[c * (steps + 1) + k]
            u = p * cosd + turn(p) * sind
            nxt = u - kap_g * jnp.dot(u.astype(BF16), gram, preferred_element_type=F32)
            pall[c * (steps + 1) + k + 1, 0:s, :] = nxt[:s]
            pall[c * (steps + 1) + k + 1, s : s + 8, :] = nxt[s:] + pown[pl.ds(t, 1), :]
        return 0

    lax.fori_loop(0, steps, step, 0)

    def last(c):
        return pall[c * (steps + 1) + steps]

    for p in range(4):
        join(last(2 * p), last(2 * p + 1), comb.at[p])
    join(comb[0], comb[1], comb.at[4])
    join(comb[2], comb[3], comb.at[5])
    join(comb[4], comb[5], mcore)

    c_core = exchange(mcore, mrecv.at[0], 1, partner)
    c_core.start()
    c_core.wait()
    mine = mcore[...]
    theirs = mrecv[0]
    join(jnp.where(w == 0, mine, theirs), jnp.where(w == 0, theirs, mine), mpair)

    odd = lax.rem(r, 2)
    c_pair = exchange(mpair, mrecv.at[1], 2, {"roll": r + 1 - 2 * odd, "width": w})
    c_pair.start()
    c_pair.wait()
    mine = mpair[...]
    theirs = mrecv[1]
    join(jnp.where(odd == 0, mine, theirs), jnp.where(odd == 0, theirs, mine), mquad)

    onward = lax.rem(r + 2, n_roll)
    c_x = exchange(xsend, xrecv, 3, {"roll": onward, "width": w})

    @pl.when(r < 2)
    def _():
        xrecv[...] = jnp.broadcast_to(init_ref[...], xrecv.shape)

    @pl.when(r >= 2)
    def _():
        c_x.wait_recv()

    x = xrecv[0:1, :]
    xcol = column(x)

    @pl.when(r < n_roll - 2)
    def _():
        xsend[...] = jnp.broadcast_to(apply(xcol, mquad[...]), xsend.shape)
        c_x.start()

    x = jnp.where(odd == 1, apply(xcol, mrecv[1]), x)
    x = jnp.where(w == 1, apply(column(x), mrecv[0]), x)

    def along(c, xc):
        col = column(xc)
        val = None
        for k in range(steps):
            val = apply(col, pall[c * (steps + 1) + k + 1])
            xs[c * steps + k : c * steps + k + 1, :] = val
        return col, val

    col0, x1 = along(0, x)
    x4 = apply(col0, comb[4])
    x2 = apply(col0, comb[0])
    col4, x5 = along(4, x4)
    x6 = apply(col4, comb[2])
    _, x3 = along(2, x2)
    _, x7 = along(6, x6)
    along(1, x1)
    along(3, x3)
    along(5, x5)
    along(7, x7)

    final = jnp.logical_and(q == nq - 1, row_t == th - 1)
    xf = xs[...]
    v = jnp.where(final, xf, keep * xf)
    ar, ai = fr, fi
    hop = 1
    while hop < th:
        later = jnp.where(row_t < th - hop, pltpu.roll(v, th - hop, 0), 0.0)
        v = v + later * ar + turn(later) * (ai * sgn)
        ar, ai = ar * ar - ai * ai, 2.0 * ar * ai
        hop *= 2

    bsend[...] = jnp.broadcast_to(v[0:1, :], bsend.shape)

    def away(d):
        return pltpu.make_async_remote_copy(
            src_ref=bsend, dst_ref=brecv.at[d - 1], send_sem=b_ss.at[d - 1], recv_sem=b_rs.at[d - 1],
            device_id=at(lax.rem(q - d + nq, nq)), device_id_type=MESH,
        )

    def send_b(d, _):
        @pl.when(q >= d)
        def _():
            away(d).start()

        return 0

    def recv_b(d, _):
        @pl.when(q + d < nq)
        def _():
            away(d).wait_recv()

        return 0

    def sent_b(d, _):
        @pl.when(q >= d)
        def _():
            away(d).wait_send()

        return 0

    brecv[nq - 1] = jnp.zeros(brecv.shape[1:], F32)

    def blank(d, _):
        @pl.when(q + d >= nq)
        def _():
            brecv[d - 1] = jnp.zeros(brecv.shape[1:], F32)

        return 0

    lax.fori_loop(1, nq, send_b, 0)
    lax.fori_loop(1, nq, blank, 0)
    lax.fori_loop(1, nq, recv_b, 0)
    late = brecv[:, 0, :]
    s_in = jnp.sum(late * far_r + turn(late) * (far_i * sgn), axis=0, keepdims=True)
    v = v + s_in * tail_r + turn(jnp.broadcast_to(s_in, (8, s)))[0:1] * (tail_i * sgn)
    ssend[...] = v
    c_s = exchange(ssend, srecv, 4, partner)
    c_s.start()
    out_ref[own_rows, :] = v
    c_s.wait()
    out_ref[oth_rows, :] = srecv[...]

    @pl.when(r < n_roll - 2)
    def _():
        c_x.wait_send()

    lax.fori_loop(1, nq, sent_b, 0)


def shards(n_roll, lines_y, defect_mask, loading, decay_rate, angle, gain, smooth_gain, initial):
    s = loading.shape[1]
    lines = lines_y.shape[0]
    th = lines // 2
    steps = th // CHAINS
    nb = loading.shape[0] // PIX_BLK
    nq = 2 * n_roll
    pixels = lines_y.shape[1] * lax.axis_size("width")
    radius = 1.0 - decay_rate
    cosr = radius * jnp.cos(angle)
    sinr = radius * jnp.sin(angle)
    one = jnp.ones_like(gain)
    keep = 1.0 - smooth_gain * radius * radius

    left = jnp.stack([
        cosr, -sinr, gain / pixels, gain * (math.sqrt(s) / pixels),
        smooth_gain * cosr, -(smooth_gain * sinr), keep, -one,
    ])
    right = jnp.stack([
        cosr, sinr, gain / pixels, gain * (math.sqrt(s) / pixels),
        smooth_gain * cosr, -(smooth_gain * sinr), keep, one,
    ])
    par = jnp.concatenate([left, right], axis=1)
    vm = pl.BlockSpec(memory_space=pltpu.VMEM)
    smoothed = pl.pallas_call(
        functools.partial(kernel, n_roll),
        out_shape=jax.ShapeDtypeStruct((lines, s), F32),
        in_specs=[vm] * 5,
        out_specs=vm,
        scratch_shapes=[
            pltpu.VMEM((nb * s, s), F32),
            pltpu.VMEM((s * th, s), F32),
            pltpu.VMEM((s * th, s), F32),
            pltpu.VMEM((s * th, s), F32),
            pltpu.VMEM((lines, s), F32),
            pltpu.VMEM((th, s), F32),
            pltpu.VMEM((th, s), F32),
            pltpu.VMEM((CHAINS * (steps + 1), s + 8, s), F32),
            pltpu.VMEM((6, s + 8, s), F32),
            pltpu.VMEM((s + 8, s), F32),
            pltpu.VMEM((s + 8, s), F32),
            pltpu.VMEM((s + 8, s), F32),
            pltpu.VMEM((2, s + 8, s), F32),
            pltpu.VMEM((th, s), F32),
            pltpu.VMEM((8, s), F32),
            pltpu.VMEM((8, s), F32),
            pltpu.VMEM((8, s), F32),
            pltpu.VMEM((nq, 8, s), F32),
            pltpu.VMEM((th, s), F32),
            pltpu.VMEM((th, s), F32),
            pltpu.SemaphoreType.DMA((PIECES,)),
            pltpu.SemaphoreType.DMA((PIECES,)),
            pltpu.SemaphoreType.DMA((5,)),
            pltpu.SemaphoreType.DMA((5,)),
            pltpu.SemaphoreType.DMA((nq,)),
            pltpu.SemaphoreType.DMA((nq,)),
        ],
        compiler_params=pltpu.CompilerParams(
            collective_id=0, has_side_effects=True, vmem_limit_bytes=48 * 1024 * 1024
        ),
        name="filter_smoother",
    )(lines_y, defect_mask, loading, par, initial.reshape(1, s))
    image_rows = lax.dot_general(
        smoothed.astype(BF16), loading, (((1,), (1,)), ((), ())), preferred_element_type=F32
    )
    background = (image_rows * (1.0 / math.sqrt(s))).astype(BF16)
    return (smoothed, background)


def solution(mesh):
    in_specs = (
        P(("groups", "roll"), "width"),
        P(("groups", "roll"), "width"),
        P("width", None),
        P(),
        P(),
        P(),
        P(),
        P("groups"),
    )
    out_specs = (P(("groups", "roll"), None), P(("groups", "roll"), "width"))
    return jax.shard_map(
        functools.partial(shards, mesh.shape["roll"]),
        mesh=mesh, in_specs=in_specs, out_specs=out_specs, check_vma=False,
    )
```

time: 296 us -> 53.6 us (0.18); the launches traced: 292 us -> 53.3 us
  blocking collectives: 132 us -> 0 us
  matrix products: 76.1 us -> 1.96 us
  Pallas kernels: 0 us -> 43.9 us
  other arithmetic: 23.7 us -> 1.49 us
  waiting for transfers between devices: 22.2 us -> 0 us
  local copies, waits for them, and re-layouts: 22.6 us -> 5.26 us
  between operations: 15.3 us -> 0.66 us
    all_gather x5 -> x0, blocking collectives: 128 us -> none  [entering(): gathered = jax.tree.map(lambda a: lax.all_gather(a, axis), part)]
    dot_general x27 -> x1, matrix products: 76.1 us -> 1.96 us  [shards(): lax.dot_general(smoothed.astype(BF16), loading, (((1,), (1,)), ((), ())),...]
    pallas_call x0 -> x1, Pallas kernels: none -> 43.9 us  [shards(): pl.pallas_call(functools.partial(kernel, n_roll), out_shape=jax.ShapeDtyp...]
    psum x1 -> x0, waiting for transfers between devices: 22.2 us -> none  [shards(): gram_rows, projected = lax.psum((gram_part, proj_part), 'width')]
    slice x89 -> x0, local copies, waits for them, and re-layouts: 13.5 us -> none  [the longest x64 5.49 us: shards(): acc_re, acc_im, acc_off = lax.associative_scan(join_back, flipped)]
    add x39 -> x0, other arithmetic: 11.8 us -> none  [the longest x1 7.83 us: shards(): left_cols * cos_part + right_cols * sin_part]
    concatenate x45 -> x1, other arithmetic: 6.17 us -> 0.08 us  [shards(): par = jnp.concatenate([left, right], axis=1)]
    psum x1 -> x0, blocking collectives: 3.86 us -> none  [shards(): gram_rows, projected = lax.psum((gram_part, proj_part), 'width')]
  transfers between devices with their start and end apart: 1 -> 0, of which waited for: 1 -> 0; matrix products, arithmetic and copies ran while one was open for 4% -> 0% of each run, Pallas kernels for 0% -> 0%
where the time goes in v1:
time: 53.6 us; the launch traced here: 53.3 us
  Pallas kernels  43.9 us (82%)
  local copies, waits for them, and re-layouts  5.26 us (10%)
  matrix products  1.96 us (4%)
  other arithmetic  1.49 us (3%)
  between operations  0.66 us (1%)
    pallas_call x1, Pallas kernels, shards(): pl.pallas_call(functools.partial(kernel, n_roll), out_shape=jax.ShapeDtyp...  43.9 us
    unnamed x8, local copies, waits for them, and re-layouts  5.21 us
    dot_general x1, matrix products, shards(): lax.dot_general(smoothed.astype(BF16), loading, (((1,), (1,)), ((), ())),...  1.96 us
    another operation x2, other arithmetic, shards(): jnp.stack([cosr, -sinr, gain / pixels, gain * (math.sqrt(s) / pixels), sm...  1.41 us

profile of v1, /device:TPU:0, one launch (start us, length us, event | category | flops | bytes accessed | tf_op | source)
XLA Modules:
  0.0 53.3 jit_solution(14710148098253970201)
XLA Ops:
  0.6 0.7 %fusion.3 = (f32[1,64]{1,0:T(1,128)S(1)}, f32[1,64]{1,0:T(1,128)S(1)}, f32[1,64]{1,0:T(1,128)S(1)}, f32[64]{0:T(128)S(1)}, f32[1,64]{1,0:T(1,128)S(1)}) fusion(f32[64]{0:T(128)} %param.14, f32[64]{0:T(128)} %param.11, f32[64]{0:T(128)} %param.12), kind=kLoop, calls=%fused_computation.13 | loop fusion | flops 512 | bytes 2048 | tf_op jit(solution)/shard_map/stack | solution.py:332
  1.4 0.7 %multiply_bitcast_fusion.1 = (f32[1,64]{1,0:T(1,128)S(1)}, f32[1,64]{1,0:T(1,128)S(1)}, f32[1,64]{1,0:T(1,128)S(1)}) fusion(f32[64]{0:T(128)} %param.13, f32[64]{0:T(128)} %param.14, f32[64]{0:T(128)S(1)} %get-tuple-element.7), kind=kLoop, calls=%fused_computation.8 | loop fusion | flops 256 | bytes 1536 | tf_op jit(solution)/shard_map/stack | solution.py:332
  2.1 0.1 pad_maximum_fusion.par_ref
  2.2 0.8 %copy.10.mask_ref = s32[112,64]{1,0:T(8,128)S(1)} copy(s32[112,64]{0,1:T(8,128)} %param.9) | data formatting | bytes 57344 | tf_op args[1]
  3.0 0.0 copy-start
  3.0 1.6 %copy-done = bf16[8192,128]{1,0:T(8,128)(2,1)S(1)} copy-done((bf16[8192,128]{1,0:T(8,128)(2,1)S(1)}, bf16[8192,128]{1,0:T(8,128)(2,1)}, u32[]{:S(2)}) %copy-start) | copy-done | bytes 2097176
  4.6 0.0 copy-start.1
  4.6 1.5 %copy-done.1 = bf16[112,8192]{1,0:T(8,128)(2,1)S(1)} copy-done((bf16[112,8192]{1,0:T(8,128)(2,1)S(1)}, bf16[112,8192]{1,0:T(8,128)(2,1)}, u32[]{:S(2)}) %copy-start.1) | copy-done | bytes 1835032
  6.1 0.0 copy-start.2
  6.1 0.7 %copy-done.2 = f32[128]{0:T(128)S(1)} copy-done((f32[128]{0:T(128)S(1)}, f32[128]{0:T(128)}, u32[]{:S(2)}) %copy-start.2) | copy-done | bytes 536
  6.8 43.9 %filter_smoother.1 = f32[112,128]{1,0:T(8,128)S(1)} custom-call(bf16[112,8192]{1,0:T(8,128)(2,1)S(1)} %copy-done.1, s32[112,64]{1,0:T(8,128)S(1)} %copy.10.mask_ref, bf16[8192,128]{1,0:T(8,128)(2,1)S(1)} %copy-done, f32[8,128]{1,0:T(8,128)S(1)} %pad_maximum_fusion.par_ref, f32[1,128]{1,0:T(1,128)S(1)} %bitcast.17), custom_call_target="tpu_custom_call" | custom-call | tf_op jit(solution)/shard_map/filter_smoother/pallas_call | solution.py:342
  50.7 2.0 %fusion = bf16[112,8192]{1,0:T(8,128)(2,1)} fusion(bf16[8192,128]{1,0:T(8,128)(2,1)S(1)} %copy-done, f32[112,128]{1,0:T(8,128)S(1)} %filter_smoother.1), kind=kOutput, calls=%fused_computation.1 | convolution fusion | flops 236730368 | bytes 3989504 | tf_op jit(solution)/shard_map/dot_general | solution.py:380
  52.7 0.6 %copy.12 = f32[112,128]{1,0:T(8,128)} copy(f32[112,128]{1,0:T(8,128)S(1)} %filter_smoother.1) | data formatting | bytes 114688
  (4 shorter events, 0.1 us)
Async XLA Ops:
  3.0 1.6 %copy-start = (bf16[8192,128]{1,0:T(8,128)(2,1)S(1)}, bf16[8192,128]{1,0:T(8,128)(2,1)}, u32[]{:S(2)}) copy-start(bf16[8192,128]{1,0:T(8,128)(2,1)} %load_ref.1) | copy-start | bytes 6291460
  4.6 1.5 %copy-start.1 = (bf16[112,8192]{1,0:T(8,128)(2,1)S(1)}, bf16[112,8192]{1,0:T(8,128)(2,1)}, u32[]{:S(2)}) copy-start(bf16[112,8192]{1,0:T(8,128)(2,1)} %y_ref.1) | copy-start | bytes 5505028
  6.1 0.7 %copy-start.2 = (f32[128]{0:T(128)S(1)}, f32[128]{0:T(128)}, u32[]{:S(2)}) copy-start(f32[128]{0:T(128)} %param.15) | copy-start | bytes 1540

commit v2 on v1

v2 whole, which is shorter than its diff:
```python
import functools
import math

import jax
import jax.numpy as jnp
from jax import lax
from jax.experimental import pallas as pl
from jax.experimental.pallas import tpu as pltpu
from jax.sharding import PartitionSpec as P

PIX_BLK = 128
CHAINS = 8
PIECES = 8
MESH = pl.DeviceIdType.MESH
HI = lax.Precision.HIGHEST
F32 = jnp.float32
BF16 = jnp.bfloat16


def turn(v):
    return pltpu.roll(v, v.shape[-1] // 2, 1)


def join(first, second, dst):
    s = second.shape[1]
    r = jnp.dot(first, second[:s], precision=HI, preferred_element_type=F32)
    dst[0:s, :] = r[:s]
    dst[s : s + 8, :] = r[s:] + second[s:]


def column(x):
    return jnp.broadcast_to(x, (x.shape[1], x.shape[1])).T


def apply(xcol, m):
    s = xcol.shape[0]
    return jnp.sum(m[:s] * xcol, axis=0, keepdims=True) + m[s : s + 1]


def powers(fr, fi, expo, bits):
    tr = jnp.ones(expo.shape, F32)
    ti = jnp.zeros(expo.shape, F32)
    for k in range(bits):
        on = (expo >> k) & 1 == 1
        nr = tr * fr - ti * fi
        ni = tr * fi + ti * fr
        tr = jnp.where(on, nr, tr)
        ti = jnp.where(on, ni, ti)
        fr, fi = fr * fr - fi * fi, 2.0 * fr * fi
    return tr, ti


def kernel(
    n_roll, y_hbm, maskt_hbm, load_hbm, decay_hbm, angle_hbm, gain_hbm, sgain_hbm, init_hbm, out_ref,
    y_ref, load_ref, maskt_ref, par_in, init_ref,
    mfull, mrem, bs, gown, pacc, precv, pown, pall, comb, mcore, mpair, mquad, mrecv, xs,
    xsend, xrecv, bsend, bquad, brows, zsend, zrecv, ssend, srecv,
    in_s, small_s, g_ss, g_rs, one_ss, one_rs, b_ss, b_rs, z_ss, z_rs,
):
    s = load_ref.shape[1]
    half = s // 2
    lines = y_ref.shape[0]
    th = lines // 2
    steps = th // CHAINS
    nb = load_ref.shape[0] // PIX_BLK
    pixels = 2 * load_ref.shape[0]
    nq = 2 * n_roll
    nz = n_roll // 2
    r = lax.axis_index("roll")
    w = lax.axis_index("width")
    q = 2 * r + w
    other = 1 - w
    wide = load_ref.shape[0] // PIECES

    smalls = [
        pltpu.make_async_copy(src, dst, small_s.at[k])
        for k, (src, dst) in enumerate([
            (maskt_hbm, maskt_ref), (decay_hbm, par_in.at[0]), (angle_hbm, par_in.at[1]),
            (gain_hbm, par_in.at[2]), (sgain_hbm, par_in.at[3]), (init_hbm, init_ref),
        ])
    ]
    for cp in smalls:
        cp.start()
    loads = []
    for c in range(PIECES):
        span = pl.ds(c * wide, wide)
        pair = (
            pltpu.make_async_copy(load_hbm.at[span, :], load_ref.at[span, :], in_s.at[0, c]),
            pltpu.make_async_copy(y_hbm.at[:, span], y_ref.at[:, span], in_s.at[1, c]),
        )
        for cp in pair:
            cp.start()
        loads.append(pair)

    def at(place):
        return {"roll": lax.div(place, 2), "width": lax.rem(place, 2)}

    barrier = pltpu.get_barrier_semaphore()

    def greet(d, _):
        pl.semaphore_signal(barrier, inc=1, device_id=at(lax.rem(q + d, nq)), device_id_type=MESH)
        return 0

    lax.fori_loop(1, nq, greet, 0)
    for cp in smalls:
        cp.wait()

    eye = jnp.where(
        lax.broadcasted_iota(jnp.int32, (nb, nb), 0) == lax.broadcasted_iota(jnp.int32, (nb, nb), 1),
        1.0, 0.0,
    ).astype(BF16)
    m_f = lax.dot_general(
        maskt_ref[...].astype(F32).astype(BF16), eye, (((0,), (0,)), ((), ())),
        preferred_element_type=F32,
    )
    mfull[...] = m_f
    m_all = m_f.astype(BF16)

    own_rows = pl.ds(pl.multiple_of(w * th, 8), th)
    oth_rows = pl.ds(pl.multiple_of(other * th, 8), th)

    def exchange(src, dst, k, dev):
        return pltpu.make_async_remote_copy(
            src_ref=src, dst_ref=dst, send_sem=one_ss.at[k], recv_sem=one_rs.at[k],
            device_id=dev, device_id_type=MESH,
        )

    partner = {"roll": r, "width": other}
    c_mask = exchange(mfull.at[oth_rows, :], mrem, 5, partner)

    pacc[...] = jnp.zeros_like(pacc)
    per = 4
    few = nb // PIECES
    copies = []
    for c in range(PIECES):
        for cp in loads[c]:
            cp.wait()

        def blocks(g, _):
            b0 = c * few + g * per
            rows = pl.ds(pl.multiple_of(b0 * PIX_BLK, per * PIX_BLK), per * PIX_BLK)
            hh = load_ref[rows, :]
            for k in range(per):
                h = hh[k * PIX_BLK : (k + 1) * PIX_BLK]
                bs[pl.ds(pl.multiple_of((b0 + k) * s, s), s), :] = lax.dot_general(
                    h, h, (((0,), (0,)), ((), ())), preferred_element_type=F32
                )
            shape = (nb, per * PIX_BLK)
            pick = jnp.where(
                lax.broadcasted_iota(jnp.int32, shape, 0)
                == b0 + lax.broadcasted_iota(jnp.int32, shape, 1) // PIX_BLK,
                1.0, 0.0,
            ).astype(BF16)
            mb = jnp.dot(m_all, pick, preferred_element_type=F32).astype(BF16)
            pacc[...] += jnp.dot(y_ref[:, rows] * mb, hh, preferred_element_type=F32)
            return 0

        lax.fori_loop(0, few // per, blocks, 0)
        if c == 0:
            pl.semaphore_wait(barrier, nq - 1)
            c_mask.start()
        cp = pltpu.make_async_remote_copy(
            src_ref=bs.at[pl.ds(c * few * s, few * s), :],
            dst_ref=bs.at[pl.ds((nb + c * few) * s, few * s), :],
            send_sem=g_ss.at[c], recv_sem=g_rs.at[c], device_id=partner, device_id_type=MESH,
        )
        cp.start()
        copies.append(cp)

    c_proj = exchange(pacc.at[oth_rows, :], precv, 0, partner)
    c_proj.start()

    decay = par_in[0]
    angle = par_in[1]
    gain = par_in[2]
    sgain = par_in[3]
    radius = 1.0 - decay
    cosr = radius * jnp.cos(angle)
    sinr = radius * jnp.sin(angle)
    keep_h = 1.0 - sgain * radius * radius

    def both(a, b):
        return jnp.concatenate([a, b], axis=1)

    cosd = both(cosr, cosr)
    sind = both(-sinr, sinr)
    kap_g = both(gain, gain) * (1.0 / pixels)
    kap_p = both(gain, gain) * (math.sqrt(s) / pixels)
    fr = both(sgain * cosr, sgain * cosr)
    fi = both(-(sgain * sinr), -(sgain * sinr))
    keep = both(keep_h, keep_h)
    sgn = jnp.where(lax.broadcasted_iota(jnp.int32, (1, s), 1) < half, -1.0, 1.0)

    odd = lax.rem(r, 2)
    zq = lax.div(r, 2)
    kq = 2 * odd + w
    row_t = lax.broadcasted_iota(jnp.int32, (th, s), 0)
    tail_r, tail_i = powers(fr, fi, th - row_t, th.bit_length())
    cr, ci = tail_r[0:1], tail_i[0:1]
    row_k = lax.broadcasted_iota(jnp.int32, (8, s), 0)
    in_quad = row_k < 4
    qr, qi = powers(cr, ci, row_k, 3)
    qr, qi = jnp.where(in_quad, qr, 0.0), jnp.where(in_quad, qi, 0.0)
    beyond = jnp.logical_and(in_quad, row_k > kq)
    lr, li = powers(cr, ci, jnp.maximum(row_k - kq - 1, 0), 3)
    lr, li = jnp.where(beyond, lr, 0.0), jnp.where(beyond, li, 0.0)
    rest_r, rest_i = powers(cr, ci, 3 - kq + 0 * row_k, 2)
    c4r, c4i = powers(cr, ci, 4 + 0 * row_k, 3)
    row_z = lax.broadcasted_iota(jnp.int32, (zrecv.shape[0], s), 0)
    far_r, far_i = powers(c4r[0:1], c4i[0:1], row_z, zrecv.shape[0].bit_length())

    ident = jnp.where(
        lax.broadcasted_iota(jnp.int32, (s + 8, s), 0) == lax.broadcasted_iota(jnp.int32, (s + 8, s), 1),
        1.0, 0.0,
    )
    for c in range(CHAINS):
        pall[c * (steps + 1)] = ident
    bquad[...] = jnp.zeros_like(bquad)
    brows[...] = jnp.zeros_like(brows)

    def blank(d, _):
        @pl.when(zq + d >= nz)
        def _():
            zrecv[d - 1] = jnp.zeros(zrecv.shape[1:], F32)

        return 0

    lax.fori_loop(1, zrecv.shape[0] + 1, blank, 0)

    c_mask.wait()
    m_two = both(mfull[own_rows, :], mrem[...]).astype(BF16)
    c_proj.wait()
    pown[...] = (pacc[own_rows, :] + precv[...]) * kap_p
    for cp in copies:
        cp.wait()

    def rows_of(g, _):
        for k in range(2):
            i = 2 * (2 * g + k)
            b0 = bs[pl.ds(i, 2 * nb, stride=s), :]
            b1 = bs[pl.ds(i + 1, 2 * nb, stride=s), :]
            res = jnp.dot(m_two, both(b0, b1).astype(BF16), preferred_element_type=F32)
            gown[pl.ds(pl.multiple_of(i * th, 8), th), :] = res[:, :s]
            gown[pl.ds(pl.multiple_of((i + 1) * th, 8), th), :] = res[:, s:]
        return 0

    lax.fori_loop(0, s // 4, rows_of, 0)

    def step(k, _):
        for c in range(CHAINS):
            t = c * steps + k
            gram = gown[pl.ds(t, s, stride=th), :].astype(BF16)
            p = pall[c * (steps + 1) + k]
            u = p * cosd + turn(p) * sind
            nxt = u - kap_g * jnp.dot(u.astype(BF16), gram, preferred_element_type=F32)
            pall[c * (steps + 1) + k + 1, 0:s, :] = nxt[:s]
            pall[c * (steps + 1) + k + 1, s : s + 8, :] = nxt[s:] + pown[pl.ds(t, 1), :]
        return 0

    lax.fori_loop(0, steps, step, 0)

    def last(c):
        return pall[c * (steps + 1) + steps]

    for p in range(4):
        join(last(2 * p), last(2 * p + 1), comb.at[p])
    join(comb[0], comb[1], comb.at[4])
    join(comb[2], comb[3], comb.at[5])
    join(comb[4], comb[5], mcore)

    c_core = exchange(mcore, mrecv.at[0], 1, partner)
    c_core.start()
    c_core.wait()
    mine = mcore[...]
    theirs = mrecv[0]
    join(jnp.where(w == 0, mine, theirs), jnp.where(w == 0, theirs, mine), mpair)

    c_pair = exchange(mpair, mrecv.at[1], 2, {"roll": r + 1 - 2 * odd, "width": w})
    c_pair.start()
    c_pair.wait()
    mine = mpair[...]
    theirs = mrecv[1]
    join(jnp.where(odd == 0, mine, theirs), jnp.where(odd == 0, theirs, mine), mquad)

    onward = lax.rem(r + 2, n_roll)
    c_x = exchange(xsend, xrecv, 3, {"roll": onward, "width": w})

    @pl.when(r < 2)
    def _():
        xrecv[...] = jnp.broadcast_to(init_ref[...], xrecv.shape)

    @pl.when(r >= 2)
    def _():
        c_x.wait_recv()

    x = xrecv[0:1, :]
    xcol = column(x)

    @pl.when(r < n_roll - 2)
    def _():
        xsend[...] = jnp.broadcast_to(apply(xcol, mquad[...]), xsend.shape)
        c_x.start()

    x = jnp.where(odd == 1, apply(xcol, mrecv[1]), x)
    x = jnp.where(w == 1, apply(column(x), mrecv[0]), x)

    def along(c, xc):
        col = column(xc)
        val = None
        for k in range(steps):
            val = apply(col, pall[c * (steps + 1) + k + 1])
            xs[c * steps + k : c * steps + k + 1, :] = val
        return col, val

    col0, x1 = along(0, x)
    x4 = apply(col0, comb[4])
    x2 = apply(col0, comb[0])
    col4, x5 = along(4, x4)
    x6 = apply(col4, comb[2])
    _, x3 = along(2, x2)
    _, x7 = along(6, x6)
    along(1, x1)
    along(3, x3)
    along(5, x5)
    along(7, x7)

    final = jnp.logical_and(q == nq - 1, row_t == th - 1)
    xf = xs[...]
    v = jnp.where(final, xf, keep * xf)
    ar, ai = fr, fi
    hop = 1
    while hop < th:
        later = jnp.where(row_t < th - hop, pltpu.roll(v, th - hop, 0), 0.0)
        v = v + later * ar + turn(later) * (ai * sgn)
        ar, ai = ar * ar - ai * ai, 2.0 * ar * ai
        hop *= 2

    b_own = v[0:1, :]
    bsend[...] = jnp.broadcast_to(b_own, bsend.shape)

    def quad_copy(e):
        to = lax.rem(kq + e, 4)
        return pltpu.make_async_remote_copy(
            src_ref=bsend, dst_ref=bquad.at[e - 1], send_sem=b_ss.at[e - 1], recv_sem=b_rs.at[e - 1],
            device_id={"roll": 2 * zq + lax.div(to, 2), "width": lax.rem(to, 2)}, device_id_type=MESH,
        )

    trio = [quad_copy(e) for e in (3, 2, 1)]
    for cp in trio:
        cp.start()
    brows[pl.ds(kq, 1), :] = b_own
    for cp in trio:
        cp.wait_recv()
    for e in (1, 2, 3):
        brows[pl.ds(lax.rem(kq - e + 4, 4), 1), :] = bquad[e - 1, 0:1, :]
    bq = brows[...]
    bq_t = turn(bq) * sgn
    zsend[...] = jnp.broadcast_to(jnp.sum(bq * qr + bq_t * qi, axis=0, keepdims=True), zsend.shape)

    def away(d):
        return pltpu.make_async_remote_copy(
            src_ref=zsend, dst_ref=zrecv.at[d - 1], send_sem=z_ss.at[d - 1], recv_sem=z_rs.at[d - 1],
            device_id={"roll": lax.rem(r - 2 * d + n_roll, n_roll), "width": w}, device_id_type=MESH,
        )

    def send_b(d, _):
        @pl.when(zq >= nz - d)
        def _():
            away(nz - d).start()

        return 0

    def recv_b(d, _):
        @pl.when(zq + d < nz)
        def _():
            away(d).wait_recv()

        return 0

    def sent_b(d, _):
        @pl.when(zq >= d)
        def _():
            away(d).wait_send()

        return 0

    lax.fori_loop(1, nz, send_b, 0)
    near = jnp.sum(bq * lr + bq_t * li, axis=0, keepdims=True)
    lax.fori_loop(1, nz, recv_b, 0)
    late = zrecv[:, 0, :]
    s_z = jnp.sum(late * far_r + turn(late) * (far_i * sgn), axis=0, keepdims=True)
    s_z = jnp.broadcast_to(s_z, (8, s))
    s_in = near + s_z * rest_r + turn(s_z) * (rest_i * sgn)
    v = v + s_in[0:1] * tail_r + turn(s_in)[0:1] * (tail_i * sgn)
    ssend[...] = v
    c_s = exchange(ssend, srecv, 4, partner)
    c_s.start()
    out_ref[own_rows, :] = v
    c_s.wait()
    out_ref[oth_rows, :] = srecv[...]

    @pl.when(r < n_roll - 2)
    def _():
        c_x.wait_send()

    for cp in trio:
        cp.wait_send()
    lax.fori_loop(1, nz, sent_b, 0)


def shards(n_roll, lines_y, defect_mask, loading, decay_rate, angle, gain, smooth_gain, initial):
    s = loading.shape[1]
    lines = lines_y.shape[0]
    th = lines // 2
    steps = th // CHAINS
    nb = loading.shape[0] // PIX_BLK
    half = s // 2
    slots = max(8, n_roll // 2)
    vm = pl.BlockSpec(memory_space=pltpu.VMEM)
    smoothed = pl.pallas_call(
        functools.partial(kernel, n_roll),
        out_shape=jax.ShapeDtypeStruct((lines, s), F32),
        in_specs=[pl.BlockSpec(memory_space=pltpu.HBM)] * 8,
        out_specs=vm,
        scratch_shapes=[
            pltpu.VMEM(lines_y.shape, BF16),
            pltpu.VMEM(loading.shape, BF16),
            pltpu.VMEM((nb, lines), jnp.int32),
            pltpu.VMEM((4, 1, half), F32),
            pltpu.VMEM((1, s), F32),
            pltpu.VMEM((lines, nb), F32),
            pltpu.VMEM((th, nb), F32),
            pltpu.VMEM((2 * nb * s, s), F32),
            pltpu.VMEM((s * th, s), F32),
            pltpu.VMEM((lines, s), F32),
            pltpu.VMEM((th, s), F32),
            pltpu.VMEM((th, s), F32),
            pltpu.VMEM((CHAINS * (steps + 1), s + 8, s), F32),
            pltpu.VMEM((6, s + 8, s), F32),
            pltpu.VMEM((s + 8, s), F32),
            pltpu.VMEM((s + 8, s), F32),
            pltpu.VMEM((s + 8, s), F32),
            pltpu.VMEM((2, s + 8, s), F32),
            pltpu.VMEM((th, s), F32),
            pltpu.VMEM((8, s), F32),
            pltpu.VMEM((8, s), F32),
            pltpu.VMEM((8, s), F32),
            pltpu.VMEM((3, 8, s), F32),
            pltpu.VMEM((8, s), F32),
            pltpu.VMEM((8, s), F32),
            pltpu.VMEM((slots, 8, s), F32),
            pltpu.VMEM((th, s), F32),
            pltpu.VMEM((th, s), F32),
            pltpu.SemaphoreType.DMA((2, PIECES)),
            pltpu.SemaphoreType.DMA((6,)),
            pltpu.SemaphoreType.DMA((PIECES,)),
            pltpu.SemaphoreType.DMA((PIECES,)),
            pltpu.SemaphoreType.DMA((6,)),
            pltpu.SemaphoreType.DMA((6,)),
            pltpu.SemaphoreType.DMA((3,)),
            pltpu.SemaphoreType.DMA((3,)),
            pltpu.SemaphoreType.DMA((slots,)),
            pltpu.SemaphoreType.DMA((slots,)),
        ],
        compiler_params=pltpu.CompilerParams(
            collective_id=0, has_side_effects=True, vmem_limit_bytes=60 * 1024 * 1024
        ),
        name="filter_smoother",
    )(
        lines_y, defect_mask.T, loading, decay_rate.reshape(1, half), angle.reshape(1, half),
        gain.reshape(1, half), smooth_gain.reshape(1, half), initial.reshape(1, s),
    )
    image_rows = lax.dot_general(
        smoothed.astype(BF16), loading, (((1,), (1,)), ((), ())), preferred_element_type=F32
    )
    background = (image_rows * (1.0 / math.sqrt(s))).astype(BF16)
    return (smoothed, background)


def solution(mesh):
    in_specs = (
        P(("groups", "roll"), "width"),
        P(("groups", "roll"), "width"),
        P("width", None),
        P(),
        P(),
        P(),
        P(),
        P("groups"),
    )
    out_specs = (P(("groups", "roll"), None), P(("groups", "roll"), "width"))
    return jax.shard_map(
        functools.partial(shards, mesh.shape["roll"]),
        mesh=mesh, in_specs=in_specs, out_specs=out_specs, check_vma=False,
    )
```

time: 53.6 us -> 53.2 us (level)
  Pallas kernels: 43.9 us -> 48.9 us
  local copies, waits for them, and re-layouts: 5.26 us -> 0.63 us
  other arithmetic: 1.49 us -> 0 us
  matrix products: 1.96 us -> 2.83 us
    pallas_call x1, Pallas kernels: 43.9 us -> 48.9 us  [shards(): pl.pallas_call(functools.partial(kernel, n_roll), out_shape=jax.ShapeDtyp...]
    unnamed x8 -> x5, local copies, waits for them, and re-layouts: 5.21 us -> 0.63 us
    another operation x2 -> x0, other arithmetic: 1.41 us -> none  [shards(): jnp.stack([cosr, -sinr, gain / pixels, gain * (math.sqrt(s) / pixels), sm...]
    dot_general x1, matrix products: 1.96 us -> 2.83 us  [shards(): lax.dot_general(smoothed.astype(BF16), loading, (((1,), (1,)), ((), ())),...]
where the time goes in v2:
time: 53.2 us; the launch traced here: 53 us
  Pallas kernels  48.9 us (92%)
  matrix products  2.83 us (5%)
  between operations  0.67 us (1%)
  local copies, waits for them, and re-layouts  0.63 us (1%)
    pallas_call x1, Pallas kernels, shards(): pl.pallas_call(functools.partial(kernel, n_roll), out_shape=jax.ShapeDtyp...  48.9 us
    dot_general x1, matrix products, shards(): lax.dot_general(smoothed.astype(BF16), loading, (((1,), (1,)), ((), ())),...  2.83 us

profile of v2, /device:TPU:0, one launch (start us, length us, event | category | flops | bytes accessed | tf_op | source)
XLA Modules:
  0.0 53.0 jit_solution(11065335050289534906)
XLA Ops:
  0.6 0.0 copy-start
  0.6 48.9 %filter_smoother.1 = f32[112,128]{1,0:T(8,128)} custom-call(bf16[112,8192]{1,0:T(8,128)(2,1)} %y_hbm.1, s32[64,112]{1,0:T(8,128)} %bitcast.7, bf16[8192,128]{1,0:T(8,128)(2,1)} %load_hbm.1, f32[1,64]{1,0:T(1,128)} %bitcast.8, f32[1,64]{1,0:T(1,128)} %bitcast.9, f32[1,64]{1,0:T(1,128)} %bitcast.10, f32[1,64]{1,0:T(1,128)} %bitcast.11, f32[1,128]{1,0:T(1,128)} %bitcast.12), custom_call_target="tpu_custom_call" | custom-call | tf_op jit(solution)/shard_map/filter_smoother/pallas_call | solution.py:420
  49.5 0.0 copy-done
  49.5 0.0 copy-start.1
  49.5 2.8 %fusion = bf16[112,8192]{1,0:T(8,128)(2,1)} fusion(bf16[8192,128]{1,0:T(8,128)(2,1)S(1)} %copy-done, f32[112,128]{1,0:T(8,128)} %filter_smoother.1), kind=kOutput, calls=%fused_computation.1 | convolution fusion | flops 236730368 | bytes 3989504 | tf_op jit(solution)/shard_map/dot_general | solution.py:473
  52.4 0.0 copy-done.1
  52.4 0.6 %copy.11 = f32[112,128]{1,0:T(8,128)} copy(f32[112,128]{1,0:T(8,128)S(1)} %copy-done.1) | data formatting | bytes 114688
Async XLA Ops:
  0.6 48.9 %copy-start = (bf16[8192,128]{1,0:T(8,128)(2,1)S(1)}, bf16[8192,128]{1,0:T(8,128)(2,1)}, u32[]{:S(2)}) copy-start(bf16[8192,128]{1,0:T(8,128)(2,1)} %load_hbm.1) | copy-start | bytes 6291460
  49.5 2.8 %copy-start.1 = (f32[112,128]{1,0:T(8,128)S(1)}, f32[112,128]{1,0:T(8,128)}, u32[]{:S(2)}) copy-start(f32[112,128]{1,0:T(8,128)} %filter_smoother.1) | copy-start | bytes 172036

commit v3 on v2

--- a/solution.py
+++ b/solution.py
@@ -53,9 +53,9 @@
 def kernel(
     n_roll, y_hbm, maskt_hbm, load_hbm, decay_hbm, angle_hbm, gain_hbm, sgain_hbm, init_hbm, out_ref,
     y_ref, load_ref, maskt_ref, par_in, init_ref,
-    mfull, mrem, bs, gown, pacc, precv, pown, pall, comb, mcore, mpair, mquad, mrecv, xs,
-    xsend, xrecv, bsend, bquad, brows, zsend, zrecv, ssend, srecv,
-    in_s, small_s, g_ss, g_rs, one_ss, one_rs, b_ss, b_rs, z_ss, z_rs,
+    mfull, mrem, mwide, bs, gown, pacc, precv, pown, pall, comb, mcore, mpair, mquad, mrecv, xs,
+    xsend, xrecv, bsend, brecv, ssend, srecv,
+    in_s, small_s, g_ss, g_rs, one_ss, one_rs, b_ss, b_rs,
 ):
     s = load_ref.shape[1]
     half = s // 2
@@ -65,7 +65,6 @@
     nb = load_ref.shape[0] // PIX_BLK
     pixels = 2 * load_ref.shape[0]
     nq = 2 * n_roll
-    nz = n_roll // 2
     r = lax.axis_index("roll")
     w = lax.axis_index("width")
     q = 2 * r + w
@@ -142,7 +141,7 @@
             hh = load_ref[rows, :]
             for k in range(per):
                 h = hh[k * PIX_BLK : (k + 1) * PIX_BLK]
-                bs[pl.ds(pl.multiple_of((b0 + k) * s, s), s), :] = lax.dot_general(
+                bs[b0 + k] = lax.dot_general(
                     h, h, (((0,), (0,)), ((), ())), preferred_element_type=F32
                 )
             shape = (nb, per * PIX_BLK)
@@ -160,8 +159,8 @@
             pl.semaphore_wait(barrier, nq - 1)
             c_mask.start()
         cp = pltpu.make_async_remote_copy(
-            src_ref=bs.at[pl.ds(c * few * s, few * s), :],
-            dst_ref=bs.at[pl.ds((nb + c * few) * s, few * s), :],
+            src_ref=bs.at[pl.ds(c * few, few)],
+            dst_ref=bs.at[pl.ds(nb + c * few, few)],
             send_sem=g_ss.at[c], recv_sem=g_rs.at[c], device_id=partner, device_id_type=MESH,
         )
         cp.start()
@@ -192,22 +191,11 @@
     sgn = jnp.where(lax.broadcasted_iota(jnp.int32, (1, s), 1) < half, -1.0, 1.0)
 
     odd = lax.rem(r, 2)
-    zq = lax.div(r, 2)
-    kq = 2 * odd + w
     row_t = lax.broadcasted_iota(jnp.int32, (th, s), 0)
     tail_r, tail_i = powers(fr, fi, th - row_t, th.bit_length())
-    cr, ci = tail_r[0:1], tail_i[0:1]
-    row_k = lax.broadcasted_iota(jnp.int32, (8, s), 0)
-    in_quad = row_k < 4
-    qr, qi = powers(cr, ci, row_k, 3)
-    qr, qi = jnp.where(in_quad, qr, 0.0), jnp.where(in_quad, qi, 0.0)
-    beyond = jnp.logical_and(in_quad, row_k > kq)
-    lr, li = powers(cr, ci, jnp.maximum(row_k - kq - 1, 0), 3)
-    lr, li = jnp.where(beyond, lr, 0.0), jnp.where(beyond, li, 0.0)
-    rest_r, rest_i = powers(cr, ci, 3 - kq + 0 * row_k, 2)
-    c4r, c4i = powers(cr, ci, 4 + 0 * row_k, 3)
-    row_z = lax.broadcasted_iota(jnp.int32, (zrecv.shape[0], s), 0)
-    far_r, far_i = powers(c4r[0:1], c4i[0:1], row_z, zrecv.shape[0].bit_length())
+    far_r, far_i = powers(
+        tail_r[0:1], tail_i[0:1], lax.broadcasted_iota(jnp.int32, (nq, s), 0), nq.bit_length()
+    )
 
     ident = jnp.where(
         lax.broadcasted_iota(jnp.int32, (s + 8, s), 0) == lax.broadcasted_iota(jnp.int32, (s + 8, s), 1),
@@ -215,36 +203,45 @@
     )
     for c in range(CHAINS):
         pall[c * (steps + 1)] = ident
-    bquad[...] = jnp.zeros_like(bquad)
-    brows[...] = jnp.zeros_like(brows)
+    brecv[nq - 1] = jnp.zeros(brecv.shape[1:], F32)
 
     def blank(d, _):
-        @pl.when(zq + d >= nz)
+        @pl.when(q + d >= nq)
         def _():
-            zrecv[d - 1] = jnp.zeros(zrecv.shape[1:], F32)
-
-        return 0
-
-    lax.fori_loop(1, zrecv.shape[0] + 1, blank, 0)
+            brecv[d - 1] = jnp.zeros(brecv.shape[1:], F32)
+
+        return 0
+
+    lax.fori_loop(1, nq, blank, 0)
 
     c_mask.wait()
     m_two = both(mfull[own_rows, :], mrem[...]).astype(BF16)
+    spread = jnp.where(
+        lax.broadcasted_iota(jnp.int32, (2 * nb, 16 * nb), 0)
+        == lax.broadcasted_iota(jnp.int32, (2 * nb, 16 * nb), 1) // 8,
+        1.0, 0.0,
+    ).astype(BF16)
+    m_rep = jnp.dot(m_two, spread, preferred_element_type=F32)
+    lane8 = lax.broadcasted_iota(jnp.int32, m_rep.shape, 1) & 7
+    for k in range(8):
+        mwide[k * th : (k + 1) * th, :] = jnp.where(lane8 == k, m_rep, 0.0).astype(BF16)
     c_proj.wait()
     pown[...] = (pacc[own_rows, :] + precv[...]) * kap_p
     for cp in copies:
         cp.wait()
 
     def rows_of(g, _):
-        for k in range(2):
-            i = 2 * (2 * g + k)
-            b0 = bs[pl.ds(i, 2 * nb, stride=s), :]
-            b1 = bs[pl.ds(i + 1, 2 * nb, stride=s), :]
-            res = jnp.dot(m_two, both(b0, b1).astype(BF16), preferred_element_type=F32)
-            gown[pl.ds(pl.multiple_of(i * th, 8), th), :] = res[:, :s]
-            gown[pl.ds(pl.multiple_of((i + 1) * th, 8), th), :] = res[:, s:]
-        return 0
-
-    lax.fori_loop(0, s // 4, rows_of, 0)
+        i = 16 * g
+        wide_b = both(
+            bs[:, pl.ds(pl.multiple_of(i, 8), 8), :].reshape(16 * nb, s).astype(BF16),
+            bs[:, pl.ds(pl.multiple_of(i + 8, 8), 8), :].reshape(16 * nb, s).astype(BF16),
+        )
+        res = jnp.dot(mwide[...], wide_b, preferred_element_type=F32)
+        gown[pl.ds(pl.multiple_of(i * th, 8), 8 * th), :] = res[:, :s]
+        gown[pl.ds(pl.multiple_of((i + 8) * th, 8), 8 * th), :] = res[:, s:]
+        return 0
+
+    lax.fori_loop(0, s // 16, rows_of, 0)
 
     def step(k, _):
         for c in range(CHAINS):
@@ -335,63 +332,40 @@
         ar, ai = ar * ar - ai * ai, 2.0 * ar * ai
         hop *= 2
 
-    b_own = v[0:1, :]
-    bsend[...] = jnp.broadcast_to(b_own, bsend.shape)
-
-    def quad_copy(e):
-        to = lax.rem(kq + e, 4)
-        return pltpu.make_async_remote_copy(
-            src_ref=bsend, dst_ref=bquad.at[e - 1], send_sem=b_ss.at[e - 1], recv_sem=b_rs.at[e - 1],
-            device_id={"roll": 2 * zq + lax.div(to, 2), "width": lax.rem(to, 2)}, device_id_type=MESH,
-        )
-
-    trio = [quad_copy(e) for e in (3, 2, 1)]
-    for cp in trio:
-        cp.start()
-    brows[pl.ds(kq, 1), :] = b_own
-    for cp in trio:
-        cp.wait_recv()
-    for e in (1, 2, 3):
-        brows[pl.ds(lax.rem(kq - e + 4, 4), 1), :] = bquad[e - 1, 0:1, :]
-    bq = brows[...]
-    bq_t = turn(bq) * sgn
-    zsend[...] = jnp.broadcast_to(jnp.sum(bq * qr + bq_t * qi, axis=0, keepdims=True), zsend.shape)
+    bsend[...] = jnp.broadcast_to(v[0:1, :], bsend.shape)
 
     def away(d):
         return pltpu.make_async_remote_copy(
-            src_ref=zsend, dst_ref=zrecv.at[d - 1], send_sem=z_ss.at[d - 1], recv_sem=z_rs.at[d - 1],
-            device_id={"roll": lax.rem(r - 2 * d + n_roll, n_roll), "width": w}, device_id_type=MESH,
+            src_ref=bsend, dst_ref=brecv.at[d - 1], send_sem=b_ss.at[d - 1], recv_sem=b_rs.at[d - 1],
+            device_id=at(lax.rem(q - d + nq, nq)), device_id_type=MESH,
         )
 
     def send_b(d, _):
-        @pl.when(zq >= nz - d)
+        @pl.when(q >= d)
         def _():
-            away(nz - d).start()
+            away(d).start()
 
         return 0
 
     def recv_b(d, _):
-        @pl.when(zq + d < nz)
+        @pl.when(q + d < nq)
         def _():
             away(d).wait_recv()
 
         return 0
 
     def sent_b(d, _):
-        @pl.when(zq >= d)
+        @pl.when(q >= d)
         def _():
             away(d).wait_send()
 
         return 0
 
-    lax.fori_loop(1, nz, send_b, 0)
-    near = jnp.sum(bq * lr + bq_t * li, axis=0, keepdims=True)
-    lax.fori_loop(1, nz, recv_b, 0)
-    late = zrecv[:, 0, :]
-    s_z = jnp.sum(late * far_r + turn(late) * (far_i * sgn), axis=0, keepdims=True)
-    s_z = jnp.broadcast_to(s_z, (8, s))
-    s_in = near + s_z * rest_r + turn(s_z) * (rest_i * sgn)
-    v = v + s_in[0:1] * tail_r + turn(s_in)[0:1] * (tail_i * sgn)
+    lax.fori_loop(1, nq, send_b, 0)
+    lax.fori_loop(1, nq, recv_b, 0)
+    late = brecv[:, 0, :]
+    s_in = jnp.sum(late * far_r + turn(late) * (far_i * sgn), axis=0, keepdims=True)
+    v = v + s_in * tail_r + turn(jnp.broadcast_to(s_in, (8, s)))[0:1] * (tail_i * sgn)
     ssend[...] = v
     c_s = exchange(ssend, srecv, 4, partner)
     c_s.start()
@@ -403,9 +377,7 @@
     def _():
         c_x.wait_send()
 
-    for cp in trio:
-        cp.wait_send()
-    lax.fori_loop(1, nz, sent_b, 0)
+    lax.fori_loop(1, nq, sent_b, 0)
 
 
 def shards(n_roll, lines_y, defect_mask, loading, decay_rate, angle, gain, smooth_gain, initial):
@@ -415,7 +387,7 @@
     steps = th // CHAINS
     nb = loading.shape[0] // PIX_BLK
     half = s // 2
-    slots = max(8, n_roll // 2)
+    nq = 2 * n_roll
     vm = pl.BlockSpec(memory_space=pltpu.VMEM)
     smoothed = pl.pallas_call(
         functools.partial(kernel, n_roll),
@@ -430,7 +402,8 @@
             pltpu.VMEM((1, s), F32),
             pltpu.VMEM((lines, nb), F32),
             pltpu.VMEM((th, nb), F32),
-            pltpu.VMEM((2 * nb * s, s), F32),
+            pltpu.VMEM((8 * th, 16 * nb), BF16),
+            pltpu.VMEM((2 * nb, s, s), F32),
             pltpu.VMEM((s * th, s), F32),
             pltpu.VMEM((lines, s), F32),
             pltpu.VMEM((th, s), F32),
@@ -445,10 +418,7 @@
             pltpu.VMEM((8, s), F32),
             pltpu.VMEM((8, s), F32),
             pltpu.VMEM((8, s), F32),
-            pltpu.VMEM((3, 8, s), F32),
-            pltpu.VMEM((8, s), F32),
-            pltpu.VMEM((8, s), F32),
-            pltpu.VMEM((slots, 8, s), F32),
+            pltpu.VMEM((nq, 8, s), F32),
             pltpu.VMEM((th, s), F32),
             pltpu.VMEM((th, s), F32),
             pltpu.SemaphoreType.DMA((2, PIECES)),
@@ -457,10 +427,8 @@
             pltpu.SemaphoreType.DMA((PIECES,)),
             pltpu.SemaphoreType.DMA((6,)),
             pltpu.SemaphoreType.DMA((6,)),
-            pltpu.SemaphoreType.DMA((3,)),
-            pltpu.SemaphoreType.DMA((3,)),
-            pltpu.SemaphoreType.DMA((slots,)),
-            pltpu.SemaphoreType.DMA((slots,)),
+            pltpu.SemaphoreType.DMA((nq,)),
+            pltpu.SemaphoreType.DMA((nq,)),
         ],
         compiler_params=pltpu.CompilerParams(
             collective_id=0, has_side_effects=True, vmem_limit_bytes=60 * 1024 * 1024

time: 53.2 us -> 46.2 us (0.87)
  Pallas kernels: 48.9 us -> 41.9 us
    pallas_call x1, Pallas kernels: 48.9 us -> 41.9 us  [shards(): pl.pallas_call(functools.partial(kernel, n_roll), out_shape=jax.ShapeDtyp...]
where the time goes in v3:
time: 46.2 us; the launch traced here: 46 us
  Pallas kernels  41.9 us (91%)
  matrix products  2.84 us (6%)
  between operations  0.67 us (1%)
  local copies, waits for them, and re-layouts  0.63 us (1%)
    pallas_call x1, Pallas kernels, shards(): pl.pallas_call(functools.partial(kernel, n_roll), out_shape=jax.ShapeDtyp...  41.9 us
    dot_general x1, matrix products, shards(): lax.dot_general(smoothed.astype(BF16), loading, (((1,), (1,)), ((), ())),...  2.84 us

profile of v3, /device:TPU:0, one launch (start us, length us, event | category | flops | bytes accessed | tf_op | source)
XLA Modules:
  0.0 46.0 jit_solution(433103016048157792)
XLA Ops:
  0.6 0.0 copy-start
  0.6 41.9 %filter_smoother.1 = f32[112,128]{1,0:T(8,128)} custom-call(bf16[112,8192]{1,0:T(8,128)(2,1)} %y_hbm.1, s32[64,112]{1,0:T(8,128)} %bitcast.7, bf16[8192,128]{1,0:T(8,128)(2,1)} %load_hbm.1, f32[1,64]{1,0:T(1,128)} %bitcast.8, f32[1,64]{1,0:T(1,128)} %bitcast.9, f32[1,64]{1,0:T(1,128)} %bitcast.10, f32[1,64]{1,0:T(1,128)} %bitcast.11, f32[1,128]{1,0:T(1,128)} %bitcast.12), custom_call_target="tpu_custom_call" | custom-call | tf_op jit(solution)/shard_map/filter_smoother/pallas_call | solution.py:392
  42.6 0.0 copy-done
  42.6 0.0 copy-start.1
  42.6 2.8 %fusion = bf16[112,8192]{1,0:T(8,128)(2,1)} fusion(bf16[8192,128]{1,0:T(8,128)(2,1)S(1)} %copy-done, f32[112,128]{1,0:T(8,128)} %filter_smoother.1), kind=kOutput, calls=%fused_computation.1 | convolution fusion | flops 236730368 | bytes 3989504 | tf_op jit(solution)/shard_map/dot_general | solution.py:441
  45.4 0.0 copy-done.1
  45.4 0.6 %copy.11 = f32[112,128]{1,0:T(8,128)} copy(f32[112,128]{1,0:T(8,128)S(1)} %copy-done.1) | data formatting | bytes 114688
Async XLA Ops:
  0.6 41.9 %copy-start = (bf16[8192,128]{1,0:T(8,128)(2,1)S(1)}, bf16[8192,128]{1,0:T(8,128)(2,1)}, u32[]{:S(2)}) copy-start(bf16[8192,128]{1,0:T(8,128)(2,1)} %load_hbm.1) | copy-start | bytes 6291460
  42.6 2.9 %copy-start.1 = (f32[112,128]{1,0:T(8,128)S(1)}, f32[112,128]{1,0:T(8,128)}, u32[]{:S(2)}) copy-start(f32[112,128]{1,0:T(8,128)} %filter_smoother.1) | copy-start | bytes 172036

commit v4 on v3

--- a/solution.py
+++ b/solution.py
@@ -96,11 +96,22 @@
 
     barrier = pltpu.get_barrier_semaphore()
 
-    def greet(d, _):
-        pl.semaphore_signal(barrier, inc=1, device_id=at(lax.rem(q + d, nq)), device_id_type=MESH)
-        return 0
-
-    lax.fori_loop(1, nq, greet, 0)
+    def greet(roll, width):
+        pl.semaphore_signal(
+            barrier, inc=1, device_id={"roll": roll, "width": width}, device_id_type=MESH
+        )
+
+    greet(r, other)
+    greet(r + 1 - 2 * lax.rem(r, 2), w)
+
+    @pl.when(r >= 2)
+    def _():
+        greet(r - 2, w)
+
+    @pl.when(r < n_roll - 2)
+    def _():
+        greet(r + 2, w)
+
     for cp in smalls:
         cp.wait()
 
@@ -156,7 +167,8 @@
 
         lax.fori_loop(0, few // per, blocks, 0)
         if c == 0:
-            pl.semaphore_wait(barrier, nq - 1)
+            peers = 2 + jnp.where(r >= 2, 1, 0) + jnp.where(r < n_roll - 2, 1, 0)
+            pl.semaphore_wait(barrier, peers)
             c_mask.start()
         cp = pltpu.make_async_remote_copy(
             src_ref=bs.at[pl.ds(c * few, few)],

time: 46.2 us -> 44.6 us (0.965)
  Pallas kernels: 41.9 us -> 40.3 us
    pallas_call x1, Pallas kernels: 41.9 us -> 40.3 us  [shards(): pl.pallas_call(functools.partial(kernel, n_roll), out_shape=jax.ShapeDtyp...]
where the time goes in v4:
time: 44.6 us; the launch traced here: 44.4 us
  Pallas kernels  40.3 us (90%)
  matrix products  2.84 us (6%)
  between operations  0.67 us (2%)
  local copies, waits for them, and re-layouts  0.63 us (1%)
    pallas_call x1, Pallas kernels, shards(): pl.pallas_call(functools.partial(kernel, n_roll), out_shape=jax.ShapeDtyp...  40.3 us
    dot_general x1, matrix products, shards(): lax.dot_general(smoothed.astype(BF16), loading, (((1,), (1,)), ((), ())),...  2.84 us

profile of v4, /device:TPU:0, one launch (start us, length us, event | category | flops | bytes accessed | tf_op | source)
XLA Modules:
  0.0 44.4 jit_solution(15093043123152577559)
XLA Ops:
  0.6 0.0 copy-start
  0.6 40.3 %filter_smoother.1 = f32[112,128]{1,0:T(8,128)} custom-call(bf16[112,8192]{1,0:T(8,128)(2,1)} %y_hbm.1, s32[64,112]{1,0:T(8,128)} %bitcast.7, bf16[8192,128]{1,0:T(8,128)(2,1)} %load_hbm.1, f32[1,64]{1,0:T(1,128)} %bitcast.8, f32[1,64]{1,0:T(1,128)} %bitcast.9, f32[1,64]{1,0:T(1,128)} %bitcast.10, f32[1,64]{1,0:T(1,128)} %bitcast.11, f32[1,128]{1,0:T(1,128)} %bitcast.12), custom_call_target="tpu_custom_call" | custom-call | tf_op jit(solution)/shard_map/filter_smoother/pallas_call | solution.py:404
  40.9 0.0 copy-done
  40.9 0.0 copy-start.1
  41.0 2.8 %fusion = bf16[112,8192]{1,0:T(8,128)(2,1)} fusion(bf16[8192,128]{1,0:T(8,128)(2,1)S(1)} %copy-done, f32[112,128]{1,0:T(8,128)} %filter_smoother.1), kind=kOutput, calls=%fused_computation.1 | convolution fusion | flops 236730368 | bytes 3989504 | tf_op jit(solution)/shard_map/dot_general | solution.py:453
  43.8 0.0 copy-done.1
  43.8 0.6 %copy.11 = f32[112,128]{1,0:T(8,128)} copy(f32[112,128]{1,0:T(8,128)S(1)} %copy-done.1) | data formatting | bytes 114688
Async XLA Ops:
  0.6 40.3 %copy-start = (bf16[8192,128]{1,0:T(8,128)(2,1)S(1)}, bf16[8192,128]{1,0:T(8,128)(2,1)}, u32[]{:S(2)}) copy-start(bf16[8192,128]{1,0:T(8,128)(2,1)} %load_hbm.1) | copy-start | bytes 6291460
  40.9 2.9 %copy-start.1 = (f32[112,128]{1,0:T(8,128)S(1)}, f32[112,128]{1,0:T(8,128)}, u32[]{:S(2)}) copy-start(f32[112,128]{1,0:T(8,128)} %filter_smoother.1) | copy-start | bytes 172036
